TPU v7x, 128 devices: a whole 4x4x4 slice. The times are simulated.
128 devices in a mesh: lead: 2 (over z_hi), tile: 64 (over y, z_lo, x, core).
Axes of the slice: x: 4, y: 4, z: 4 (z_hi: 2, z_lo: 2; z = z_hi * 2 + z_lo), core: 2. Of those that a mesh axis runs over, the one named last changes fastest.
Arguments:
- states: float32 [2, 2, 128, 512, 128], P('lead', None, None, 'tile'), may hold values from -6 to 6
- cotangents: float32 [2, 2, 128, 512, 128], P('lead', None, None, 'tile'), may hold values from -6 to 6
- w_conv: bfloat16 [1152, 512], replicated, may hold values from -0.1875 to 0.1875
- b_conv: float32 [512], replicated, may hold values from -3 to 3
- w_out: bfloat16 [512, 128], replicated, may hold values from -0.25 to 0.25
- forcing: float32 [365, 128], replicated, may hold values from -3 to 3
- land: int32 [512, 128], P('tile'), may hold values 0 or 1
- dates: int32 [2], replicated, may hold values from 0 to 364
Outputs:
- state_grads: float32 [2, 2, 128, 512, 128], P('lead', None, None, 'tile')
- w1_grad: float32 [1152, 512], P('tile')
- w2_grad: float32 [512, 128], P('tile')
- b1_grad: float32 [512], P('tile')
Inputs may be any that keep to these rules, and one draw needn't show every extreme that they name: 1 marks an ocean column, 0 a land column.
All inputs are finite; a program needn't handle non-finite values. No bound on the sum of `land` on one device may be relied on, other than what follows from the above.
Results may differ from a plain program's by a relative error of at most 0.0056.
Values may be sent and summed in bfloat16 or wider, within the bound.
A program may use at most 128 MiB of HBM per device.

v0:
```python
import functools
import math

import jax
import jax.numpy as jnp
from jax import lax
from jax.experimental import pallas as pl
from jax.experimental.pallas import tpu as pltpu
from jax.sharding import PartitionSpec as P

MESH = pl.DeviceIdType.MESH
TANH_SCALE = 0.7978845608028654
CUBIC_TERM = 0.044715
F32 = jnp.float32
BF16 = jnp.bfloat16

C = 128
H = 512
ROWS = 8
L = 128
MB = 2
TILES = 64
BLOCKS = 8
LOCAL = 8
BROWS = 176


def remote(src, dst, send_sem, recv_sem, device):
    return pltpu.make_async_remote_copy(
        src_ref=src, dst_ref=dst, send_sem=send_sem, recv_sem=recv_sem,
        device_id=device, device_id_type=MESH,
    )


def dot(a, b):
    return jnp.dot(a, b, preferred_element_type=F32)


def dot_t(a, b):
    return lax.dot_general(a, b, (((1,), (1,)), ((), ())), preferred_element_type=F32)


def rolled(value, shift):
    return value if shift % L == 0 else pltpu.roll(value, shift % L, 1)


def kernel(
    scale,
    dates, x_hbm, cot_hbm, w_hbm, b_hbm, wo_hbm, f_hbm, land_hbm,
    out_hbm, w1_out, w2_out, b1_out,
    x_v, cot_v, w_v, wt_v, b_v, wo_v, f_v, land_v,
    bcol, shift, taps, halo_s, halo_r, hidden, slope, masked, pre, bias_acc,
    edge_s, edge_r, part, sg_s, sg_r, out_v, w1_acc, w2_acc, b_row,
    c_s, c_r, y_s, y_r, y_sum, f_s, f_r, l_s, l_r,
    in_sem, out_sem, halo_ss, halo_rs, edge_ss, edge_rs, sg_ss, sg_rs,
    c_ss, c_rs, y_ss, y_rs, f_ss, f_rs, l_ss, l_rs,
):
    lead = lax.axis_index("lead")
    tile = lax.axis_index("tile")
    core = lax.rem(tile, 2)
    local = lax.rem(tile, LOCAL)
    block = lax.div(tile, LOCAL)
    xpos = lax.div(local, 2)

    peers = [(lead, lax.rem(tile + 1, TILES)), (lead, lax.rem(tile + TILES - 1, TILES)), (1 - lead, tile)]
    peers += [(lead, lax.rem(block + k, BLOCKS) * LOCAL + local) for k in range(1, BLOCKS)]
    peers += [(lead, block * LOCAL + lax.rem(local + k, LOCAL)) for k in range(1, LOCAL)]
    barrier = pltpu.get_barrier_semaphore()
    for peer in peers:
        pl.semaphore_signal(barrier, inc=1, device_id=peer, device_id_type=MESH)

    loads = [
        pltpu.make_async_copy(src, dst, in_sem.at[i])
        for i, (src, dst) in enumerate(
            [(f_hbm, f_v), (x_hbm, x_v), (w_hbm, w_v), (b_hbm, b_v), (cot_hbm, cot_v), (land_hbm, land_v), (wo_hbm, wo_v)]
        )
    ]
    for load in loads:
        load.start()

    loads[0].wait()
    for m in range(MB):
        day = lax.rem(dates[m] + lead, f_hbm.shape[0])
        shift[m] = jnp.broadcast_to(f_v[pl.ds(day, 1), :], (C, L)).T
    loads[1].wait()
    for m in range(MB):
        for d, r in ((0, 0), (1, ROWS - 1)):
            halo_s[d, m] = (x_v[m, pl.ds(r, C, stride=ROWS), :] + shift[m]).astype(BF16)
    pl.semaphore_wait(barrier, len(peers))
    halo_up = remote(halo_s.at[0], halo_r.at[1], halo_ss.at[0], halo_rs.at[1], (lead, tile - 1))
    halo_down = remote(halo_s.at[1], halo_r.at[0], halo_ss.at[1], halo_rs.at[0], (lead, tile + 1))

    @pl.when(tile > 0)
    def _():
        halo_up.start()

    @pl.when(tile < TILES - 1)
    def _():
        halo_down.start()

    @pl.when(tile == 0)
    def _():
        halo_r[0] = jnp.zeros_like(halo_r[0])

    @pl.when(tile == TILES - 1)
    def _():
        halo_r[1] = jnp.zeros_like(halo_r[1])

    for m in range(MB):
        for r in range(ROWS):
            rounded = (x_v[m, pl.ds(r, C, stride=ROWS), :] + shift[m])
            for cs in (-1, 0, 1):
                view = rolled(rounded, -cs).astype(BF16)
                for rs in (-1, 0, 1):
                    if 0 <= r - rs < ROWS:
                        tap = 3 * (rs + 1) + cs + 1
                        taps[m, tap * C:(tap + 1) * C, (r - rs) * L:(r - rs + 1) * L] = view

    loads[2].wait()
    for i in range(9):
        for j in range(4):
            wt_v[j * 128:(j + 1) * 128, i * 128:(i + 1) * 128] = w_v[i * 128:(i + 1) * 128, j * 128:(j + 1) * 128].T
    loads[3].wait()
    for j in range(4):
        bcol[j * 128:(j + 1) * 128, :] = jnp.broadcast_to(b_v[:, j * 128:(j + 1) * 128], (L, L)).T
    pre[...] = jnp.zeros_like(pre)
    bias_acc[...] = jnp.zeros_like(bias_acc)

    @pl.when(lead == 1)
    def _():
        sg_r[...] = jnp.zeros_like(sg_r)

    for load in loads[4:]:
        load.wait()

    def halo_arrived():
        @pl.when(tile > 0)
        def _():
            halo_down.wait_recv()
            halo_up.wait_send()

        @pl.when(tile < TILES - 1)
        def _():
            halo_up.wait_recv()
            halo_down.wait_send()

        for m in range(MB):
            for d, rs, r in ((0, -1, 0), (1, 1, ROWS - 1)):
                row = halo_r[d, m].astype(F32)
                for cs in (-1, 0, 1):
                    tap = 3 * (rs + 1) + cs + 1
                    taps[m, tap * C:(tap + 1) * C, r * L:(r + 1) * L] = rolled(row, -cs).astype(BF16)

    def forward(m, j):
        cols = pl.ds(pl.multiple_of(j * 256, 256), 256)
        v = dot(wt_v[...], taps[m, :, cols])
        v = v + jnp.concatenate([bcol[...]] * 2, axis=1)
        v2 = v * v
        t = jnp.tanh(v * (TANH_SCALE * CUBIC_TERM * v2 + TANH_SCALE))
        p = 0.5 * t + 0.5
        out = v * p
        hidden[m, :, cols] = out.astype(BF16)
        slope[m, :, cols] = p + out * (1.0 - p) * (6.0 * TANH_SCALE * CUBIC_TERM * v2 + 2.0 * TANH_SCALE)

    def total_row(m, r):
        return cot_v[m, pl.ds(r, C, stride=ROWS), :] + sg_r[m, r].astype(F32)

    def pre_grads(m):
        land = land_v[...].astype(F32)
        for r in range(ROWS):
            masked[m, :, r * L:(r + 1) * L] = (total_row(m, r) * land[r:r + 1, :]).astype(BF16)

        def step(j, carry):
            cols = pl.ds(pl.multiple_of(j * 256, 256), 256)
            grad = dot(wo_v[...], masked[m, :, cols]) * slope[m, :, cols]
            bias_acc[...] += grad[:, :L] + grad[:, L:]
            pre[m, :, pl.ds(pl.multiple_of(j * 256 + 256, 256), 256)] = grad.astype(BF16)
            return carry

        lax.fori_loop(0, ROWS // 2, step, 0)

    def weight_grads(m, first):
        p = pre[m, :, 256:256 + ROWS * L]
        for g in range(3):
            term = dot_t(taps[m, g * 384:(g + 1) * 384, :], p)

            @pl.when(first)
            def _():
                w1_acc[g * 384:(g + 1) * 384, :] = term

            @pl.when(jnp.logical_not(first))
            def _():
                w1_acc[g * 384:(g + 1) * 384, :] += term

        term = dot_t(hidden[m], masked[m])

        @pl.when(first)
        def _():
            w2_acc[...] = term

        @pl.when(jnp.logical_not(first))
        def _():
            w2_acc[...] += term

    def conv_back(m, k):
        acc = jnp.zeros((3 * C, 2 * L), F32)
        for rs in (-1, 0, 1):
            start = pl.multiple_of((2 * k + 1 - rs) * L, L)
            acc = acc + dot(w_v[(rs + 1) * 384:(rs + 2) * 384, :], pre[m, :, pl.ds(start, 2 * L)])
        rows = []
        for half in range(2):
            lanes = slice(half * L, (half + 1) * L)
            rows.append(rolled(acc[:C, lanes], -1) + acc[C:2 * C, lanes] + rolled(acc[2 * C:, lanes], 1))
        return rows

    def edges(m):
        up = remote(edge_s.at[m, 0], edge_r.at[m, 1], edge_ss.at[m, 0], edge_rs.at[m, 1], (lead, tile - 1))
        down = remote(edge_s.at[m, 1], edge_r.at[m, 0], edge_ss.at[m, 1], edge_rs.at[m, 0], (lead, tile + 1))
        return up, down

    def sg_copy(m, i):
        rows = pl.ds(1 + 2 * i, 2) if isinstance(i, int) and i < 3 else None
        if rows is None:
            rows = pl.ds(0 if i == 3 else ROWS - 1, 1)
        return remote(sg_s.at[m, rows], sg_r.at[m, rows], sg_ss.at[m, i], sg_rs.at[m, i], (1 - lead, tile))

    def finish_row(m, r, grad):
        value = total_row(m, r) + grad
        out_v[m, pl.ds(r, C, stride=ROWS), :] = value
        sg_s[m, r] = value.astype(BF16)

    def input_grads(m):
        up, down = edges(m)
        top, part[0] = conv_back(m, 0)
        edge_s[m, 0] = top

        @pl.when(tile > 0)
        def _():
            up.start()

        part[1], bottom = conv_back(m, ROWS // 2)
        edge_s[m, 1] = bottom

        @pl.when(tile < TILES - 1)
        def _():
            down.start()

        for k in range(1, ROWS // 2):
            for half, grad in enumerate(conv_back(m, k)):
                finish_row(m, 2 * k - 1 + half, grad)

            @pl.when(lead == 1)
            def _():
                sg_copy(m, k - 1).start()

        for d, r in ((0, 0), (1, ROWS - 1)):
            @pl.when(tile > 0 if d == 0 else tile < TILES - 1)
            def _():
                (down if d == 0 else up).wait_recv()
                (up if d == 0 else down).wait_send()
                finish_row(m, r, part[d] + edge_r[m, d])

            @pl.when(tile == 0 if d == 0 else tile == TILES - 1)
            def _():
                finish_row(m, r, part[d])

            @pl.when(lead == 1)
            def _():
                sg_copy(m, 3 + d).start()

        pltpu.make_async_copy(out_v.at[m], out_hbm.at[m], out_sem.at[m]).start()

    def piece(b, half):
        return (
            w1_acc[pl.ds(pl.multiple_of(b * 144, 8), 144), pl.ds(pl.multiple_of(half * 256, 256), 256)],
            jnp.concatenate(
                [w2_acc[pl.ds(pl.multiple_of(b * 64 + half * 32 + q * 16, 16), 16), :] for q in range(2)], axis=1
            ),
            jnp.broadcast_to(b_row[:, pl.ds(pl.multiple_of(half * 256, 256), 256)], (16, 256)),
        )

    pair = (lead, tile + 1 - 2 * core)

    def c_copy(k):
        b = lax.rem(block + 1 + k, BLOCKS)
        return b, remote(c_s.at[b], c_r.at[b], c_ss.at[k], c_rs.at[k], pair)

    def y_copy(k):
        b = lax.rem(block + 1 + k, BLOCKS)
        return b, remote(y_s.at[b], y_r.at[k], y_ss.at[k], y_rs.at[k], (lead, b * LOCAL + local))

    def start_core_stage():
        for j in range(4):
            b_row[:, j * 128:(j + 1) * 128] = jnp.sum(bias_acc[j * 128:(j + 1) * 128, :].T, axis=0, keepdims=True)

        def step(k, carry):
            b, copy = c_copy(k)
            one, two, three = piece(b, 1 - core)
            c_s[b, :144, :] = one.astype(BF16)
            c_s[b, 144:160, :] = two.astype(BF16)
            c_s[b, 160:, :] = three.astype(BF16)
            copy.start()
            return carry

        lax.fori_loop(0, BLOCKS, step, 0)

    def sweep(it, carry):
        m = lax.rem(it, MB)
        ahead = it < MB

        @pl.when(ahead)
        def _():
            @pl.when(it == 0)
            def _():
                forward(m, 1)
                forward(m, 2)
                halo_arrived()
                forward(m, 0)
                forward(m, 3)

            @pl.when(it == 1)
            def _():
                lax.fori_loop(0, 4, lambda j, c: (forward(m, j), c)[1], 0)

        mine = jnp.where(ahead, lead == 1, lead == 0)

        @pl.when(mine)
        def _():
            @pl.when(lead == 0)
            def _():
                for i in range(5):
                    sg_copy(m, i).wait_recv()

            pre_grads(m)

        @pl.when(jnp.logical_not(ahead))
        def _():
            weight_grads(m, it == MB)

        @pl.when(it == 2 * MB - 1)
        def _():
            start_core_stage()

        @pl.when(mine)
        def _():
            input_grads(m)

        return carry

    lax.fori_loop(0, 2 * MB, sweep, 0)

    def y_step(k, carry):
        b, copy = c_copy(k)
        copy.wait_recv()
        for value, lo, hi in zip(piece(b, core), (0, 144, 160), (144, 160, BROWS)):
            value = value + c_r[b, lo:hi, :].astype(F32)
            y_sum[lo:hi, :] = value
            y_s[b, lo:hi, :] = value.astype(BF16)

        @pl.when(k < BLOCKS - 1)
        def _():
            y_copy(k)[1].start()

        return carry

    lax.fori_loop(0, BLOCKS, y_step, 0)

    for k in range(BLOCKS - 1):
        y_copy(k)[1].wait_recv()
        y_sum[...] += y_r[k].astype(F32)

    def f_copy(k):
        to = lax.rem(local + k, LOCAL)
        return remote(f_s.at[to], f_r.at[local], f_ss.at[k], f_rs.at[k], (lead, block * LOCAL + to))

    def f_landed(k):
        source = lax.rem(local + LOCAL - k, LOCAL)
        return remote(f_s.at[local], f_r.at[source], f_ss.at[k], f_rs.at[k], (lead, block * LOCAL + source))

    row_id = lax.broadcasted_iota(jnp.int32, (24, 256), 0)
    for j in range(LOCAL):
        rows = y_sum[18 * j:18 * j + 24, :]
        bias = jnp.broadcast_to(y_sum[160:161, :], (24, 256))
        lead_rows = jnp.where(row_id < 18, rows, bias)
        q = (j // 2) % 2
        tail = y_sum[144 + 8 * (j % 2):152 + 8 * (j % 2), q * 128:(q + 1) * 128]
        tail = jnp.concatenate([tail, jnp.zeros_like(tail)], axis=1)
        f_s[j] = jnp.concatenate([lead_rows, tail], axis=0).astype(BF16)
    for k in range(1, LOCAL):
        f_copy(k).start()
    f_r[local] = f_s[local]
    for k in range(1, LOCAL):
        f_landed(k).wait_recv()

    for half in range(2):
        total = f_r[half].astype(F32)
        for x in range(1, 4):
            total = total + f_r[2 * x + half].astype(F32)
        l_s[:, half * 256:(half + 1) * 256] = total
    tail_core = lax.div(xpos, 2)
    total = f_r[tail_core, 16:32, :L].astype(F32)
    for x in range(1, 4):
        total = total + f_r[2 * x + tail_core, 16:32, :L].astype(F32)
    l_s[24:32, :L] = total[8:16]

    l_copy = remote(l_s, l_r, l_ss, l_rs, (1 - lead, tile))
    l_copy.start()
    l_copy.wait_recv()
    result = (l_s[...] + l_r[...]) * scale
    w1_out[...] = result[:18]
    w2_out[...] = result[24:32, :L]
    b1 = result[18:19, :L]
    for q in range(1, 4):
        b1 = jnp.where(lax.div(tile, 16) == q, result[18:19, q * L:(q + 1) * L], b1)
    b1_out[...] = pltpu.roll(b1, lax.rem(L - 8 * lax.rem(tile, 16), L), 1)

    @pl.when(lead == 1)
    def _():
        for m in range(MB):
            for i in range(5):
                sg_copy(m, i).wait_send()

    for k in range(BLOCKS):
        c_copy(k)[1].wait_send()
    for k in range(BLOCKS - 1):
        y_copy(k)[1].wait_send()
    for k in range(1, LOCAL):
        f_copy(k).wait_send()
    l_copy.wait_send()
    for m in range(MB):
        pltpu.make_async_copy(out_v.at[m], out_hbm.at[m], out_sem.at[m]).wait()


def shards(states, cotangents, w_conv, b_conv, w_out, forcing, land, dates):
    grad_scale = 1.0 / math.sqrt(2 * MB * TILES * ROWS * L)
    any_spec = pl.BlockSpec(memory_space=pl.ANY)
    vmem_spec = pl.BlockSpec(memory_space=pltpu.VMEM)
    dma = pltpu.SemaphoreType.DMA
    flat = (MB, C * ROWS, L)
    out, w1, w2, b1 = pl.pallas_call(
        functools.partial(kernel, grad_scale),
        out_shape=(
            jax.ShapeDtypeStruct(flat, F32),
            jax.ShapeDtypeStruct((18, H), F32),
            jax.ShapeDtypeStruct((8, C), F32),
            jax.ShapeDtypeStruct((1, L), F32),
        ),
        in_specs=[pl.BlockSpec(memory_space=pltpu.SMEM)] + [any_spec] * 7,
        out_specs=(any_spec, vmem_spec, vmem_spec, vmem_spec),
        scratch_shapes=[
            pltpu.VMEM(flat, F32),
            pltpu.VMEM(flat, F32),
            pltpu.VMEM((9 * C, H), BF16),
            pltpu.VMEM((H, 9 * C), BF16),
            pltpu.VMEM((1, H), F32),
            pltpu.VMEM((H, C), BF16),
            pltpu.VMEM(forcing.shape, F32),
            pltpu.VMEM((ROWS, L), jnp.int32),
            pltpu.VMEM((H, L), F32),
            pltpu.VMEM((MB, C, L), F32),
            pltpu.VMEM((MB, 9 * C, ROWS * L), BF16),
            pltpu.VMEM((2, MB, C, L), BF16),
            pltpu.VMEM((2, MB, C, L), BF16),
            pltpu.VMEM((MB, H, ROWS * L), BF16),
            pltpu.VMEM((MB, H, ROWS * L), F32),
            pltpu.VMEM((MB, C, ROWS * L), BF16),
            pltpu.VMEM((MB, H, (ROWS + 4) * L), BF16),
            pltpu.VMEM((H, L), F32),
            pltpu.VMEM((MB, 2, C, L), F32),
            pltpu.VMEM((MB, 2, C, L), F32),
            pltpu.VMEM((2, C, L), F32),
            pltpu.VMEM((MB, ROWS, C, L), BF16),
            pltpu.VMEM((MB, ROWS, C, L), BF16),
            pltpu.VMEM(flat, F32),
            pltpu.VMEM((9 * C, H), F32),
            pltpu.VMEM((H, C), F32),
            pltpu.VMEM((1, H), F32),
            pltpu.VMEM((BLOCKS, BROWS, 256), BF16),
            pltpu.VMEM((BLOCKS, BROWS, 256), BF16),
            pltpu.VMEM((BLOCKS, BROWS, 256), BF16),
            pltpu.VMEM((BLOCKS - 1, BROWS, 256), BF16),
            pltpu.VMEM((BROWS, 256), F32),
            pltpu.VMEM((LOCAL, 32, 256), BF16),
            pltpu.VMEM((LOCAL, 32, 256), BF16),
            pltpu.VMEM((32, H), F32),
            pltpu.VMEM((32, H), F32),
            dma((7,)), dma((MB,)), dma((2,)), dma((2,)), dma((MB, 2)), dma((MB, 2)), dma((MB, 5)), dma((MB, 5)),
            dma((BLOCKS,)), dma((BLOCKS,)), dma((BLOCKS - 1,)), dma((BLOCKS - 1,)), dma((LOCAL,)), dma((LOCAL,)), dma, dma,
        ],
        compiler_params=pltpu.CompilerParams(collective_id=0, has_side_effects=True, vmem_limit_bytes=56 << 20),
    )(
        dates,
        states.reshape(flat),
        cotangents.reshape(flat),
        w_conv,
        b_conv.reshape(1, H),
        w_out,
        forcing,
        land,
    )
    return out.reshape(states.shape), w1, w2, b1[0, :8]


def solution(mesh):
    placed = (
        P("lead", None, None, "tile", None),
        P("lead", None, None, "tile", None),
        P(),
        P(),
        P(),
        P(),
        P("tile", None),
        P(),
    )
    return jax.shard_map(
        shards,
        mesh=mesh,
        in_specs=placed,
        out_specs=(
            P("lead", None, None, "tile", None),
            P("tile", None),
            P("tile", None),
            P("tile"),
        ),
        check_vma=False,
    )
```

profile of v0, /device:TPU:96, one launch (start us, length us, event | category | flops | bytes accessed | tf_op | source)
XLA Modules:
  0.0 65.1 jit_solution(15764374051270965984)
XLA Ops:
  0.6 59.8 %shard_map.111 = (f32[2,1024,128]{2,1,0:T(8,128)}, f32[18,512]{1,0:T(8,128)}, f32[8,128]{1,0:T(8,128)}, f32[1,128]{1,0:T(1,128)}) custom-call(s32[2]{0:T(128)} %dates.1, f32[2,1024,128]{2,1,0:T(8,128)} %bitcast.7, f32[2,1024,128]{2,1,0:T(8,128)} %bitcast.8, bf16[1152,512]{1,0:T(8,128)(2,1)} %w_hbm.1, f32[1,512]{1,0:T(1,128)} %bitcast.9, ...), custom_call_target="tpu_custom_call" | custom-call | tf_op jit(solution)/shard_map/pallas_call | solution.py:440
  60.4 0.0 copy-start
  60.4 0.0 copy-start.1
  60.5 1.1 %slice_bitcast_fusion = f32[8]{0:T(128)} fusion(f32[1,128]{1,0:T(1,128)} %get-tuple-element.11), kind=kLoop, calls=%fused_computation | loop fusion | bytes 64 | tf_op jit(solution)/shard_map/squeeze | solution.py:501
  61.6 2.3 %copy.15 = f32[1,2,128,8,128]{4,3,2,1,0:T(8,128)} copy(f32[1,2,128,8,128]{4,3,2,1,0:T(8,128)} %bitcast.6) | data formatting | bytes 2097152
  63.9 0.0 copy-done
  63.9 0.6 copy.16
  64.5 0.0 copy-done.1
  64.5 0.6 copy.17
Async XLA Ops:
  60.4 3.4 %copy-start = (f32[18,512]{1,0:T(8,128)S(1)}, f32[18,512]{1,0:T(8,128)}, u32[]{:S(2)}) copy-start(f32[18,512]{1,0:T(8,128)} %get-tuple-element.17) | copy-start | bytes 110596
  60.4 4.0 %copy-start.1 = (f32[8,128]{1,0:T(8,128)S(1)}, f32[8,128]{1,0:T(8,128)}, u32[]{:S(2)}) copy-start(f32[8,128]{1,0:T(8,128)} %get-tuple-element.18) | copy-start | bytes 12292
where the time goes:
time: 65.3 us; the launch traced here: 65.1 us
  Pallas kernels  59.8 us (92%)
  local copies, waits for them, and re-layouts  4.62 us (7%)
  between operations  0.66 us (1%)
    pallas_call x1, Pallas kernels, shards(): pl.pallas_call(functools.partial(kernel, grad_scale), out_shape=(jax.Shap...  59.8 us
    unnamed x7, local copies, waits for them, and re-layouts  3.48 us

commit v1 on v0

v1 whole, which is shorter than its diff:
```python
import functools
import math

import jax
import jax.numpy as jnp
from jax import lax
from jax.experimental import pallas as pl
from jax.experimental.pallas import tpu as pltpu
from jax.sharding import PartitionSpec as P

MESH = pl.DeviceIdType.MESH
TANH_SCALE = 0.7978845608028654
CUBIC_TERM = 0.044715
F32 = jnp.float32
BF16 = jnp.bfloat16

C = 128
H = 512
ROWS = 8
L = 128
MB = 2
TILES = 64
BLOCKS = 8
LOCAL = 8
BROWS = 176


def remote(src, dst, send_sem, recv_sem, device):
    return pltpu.make_async_remote_copy(
        src_ref=src, dst_ref=dst, send_sem=send_sem, recv_sem=recv_sem,
        device_id=device, device_id_type=MESH,
    )


def dot(a, b):
    return jnp.dot(a, b, preferred_element_type=F32)


def dot_t(a, b):
    return lax.dot_general(a, b, (((1,), (1,)), ((), ())), preferred_element_type=F32)


def rolled(value, shift):
    return value if shift % L == 0 else pltpu.roll(value, shift % L, 1)


def kernel(
    scale,
    dates, x_hbm, cot_hbm, w_hbm, b_hbm, wo_hbm, f_hbm, land_hbm,
    out_v, w1_out, w2_out, b1_out,
    x_v, cot_v, w_v, wt_v, w_cat, w_edge, b_v, wo_v, f_v, land_v,
    bcol, shift, taps, halo_s, halo_r, hidden, slope, masked, pre, bias_acc,
    edge_s, edge_r, part, sg_s, sg_r, w1_acc, w2_acc, b_row,
    c_s, c_r, y_s, y_r, y_sum, f_t, f_s, f_r, l_s, l_r,
    in_sem, halo_ss, halo_rs, edge_ss, edge_rs, sg_ss, sg_rs,
    c_ss, c_rs, y_ss, y_rs, f_ss, f_rs, l_ss, l_rs,
):
    lead = lax.axis_index("lead")
    tile = lax.axis_index("tile")
    core = lax.rem(tile, 2)
    local = lax.rem(tile, LOCAL)
    block = lax.div(tile, LOCAL)
    xpos = lax.div(local, 2)

    peers = [(lead, lax.rem(tile + 1, TILES)), (lead, lax.rem(tile + TILES - 1, TILES)), (1 - lead, tile)]
    peers += [(lead, lax.rem(block + k, BLOCKS) * LOCAL + local) for k in range(1, BLOCKS)]
    peers += [(which, block * LOCAL + lax.rem(local + k, LOCAL)) for k in range(1, LOCAL) for which in (lead, 1 - lead)]
    barrier = pltpu.get_barrier_semaphore()
    for peer in peers:
        pl.semaphore_signal(barrier, inc=1, device_id=peer, device_id_type=MESH)

    loads = [
        pltpu.make_async_copy(src, dst, in_sem.at[i])
        for i, (src, dst) in enumerate(
            [(f_hbm, f_v), (x_hbm, x_v), (w_hbm, w_v), (b_hbm, b_v), (cot_hbm, cot_v), (land_hbm, land_v), (wo_hbm, wo_v)]
        )
    ]
    for load in loads:
        load.start()

    loads[0].wait()
    for m in range(MB):
        day = lax.rem(dates[m] + lead, f_hbm.shape[0])
        shift[m] = jnp.broadcast_to(f_v[pl.ds(day, 1), :], (C, L)).T
    loads[1].wait()
    for m in range(MB):
        for d, r in ((0, 0), (1, ROWS - 1)):
            halo_s[d, m] = (x_v[m, pl.ds(r, C, stride=ROWS), :] + shift[m]).astype(BF16)
    for m in range(MB):
        for r in range(ROWS):
            rounded = (x_v[m, pl.ds(r, C, stride=ROWS), :] + shift[m])
            for cs in (-1, 0, 1):
                view = rolled(rounded, -cs).astype(BF16)
                for rs in (-1, 0, 1):
                    if 0 <= r - rs < ROWS:
                        tap = 3 * (rs + 1) + cs + 1
                        taps[m, tap * C:(tap + 1) * C, (r - rs) * L:(r - rs + 1) * L] = view

    loads[2].wait()
    for i in range(9):
        for j in range(4):
            wt_v[j * 128:(j + 1) * 128, i * 128:(i + 1) * 128] = w_v[i * 128:(i + 1) * 128, j * 128:(j + 1) * 128].T
    loads[3].wait()
    for j in range(4):
        bcol[j * 128:(j + 1) * 128, :] = jnp.broadcast_to(b_v[:, j * 128:(j + 1) * 128], (L, L)).T
    for rs in range(3):
        w_cat[:, rs * H:(rs + 1) * H] = w_v[rs * 384:(rs + 1) * 384, :]
        if rs != 1:
            w_edge[rs // 2 * 384:(rs // 2 + 1) * 384, :] = w_v[rs * 384:(rs + 1) * 384, :]
    pl.semaphore_wait(barrier, len(peers))
    halo_up = remote(halo_s.at[0], halo_r.at[1], halo_ss.at[0], halo_rs.at[1], (lead, tile - 1))
    halo_down = remote(halo_s.at[1], halo_r.at[0], halo_ss.at[1], halo_rs.at[0], (lead, tile + 1))

    @pl.when(tile > 0)
    def _():
        halo_up.start()

    @pl.when(tile < TILES - 1)
    def _():
        halo_down.start()

    @pl.when(tile == 0)
    def _():
        halo_r[0] = jnp.zeros_like(halo_r[0])

    @pl.when(tile == TILES - 1)
    def _():
        halo_r[1] = jnp.zeros_like(halo_r[1])

    for lanes in (slice(0, L), slice((ROWS + 1) * L, (ROWS + 2) * L)):
        pre[:, :, lanes] = jnp.zeros((MB, H, L), BF16)
    bias_acc[...] = jnp.zeros_like(bias_acc)

    @pl.when(lead == 1)
    def _():
        sg_r[...] = jnp.zeros_like(sg_r)

    for load in loads[4:]:
        load.wait()

    def halo_arrived():
        @pl.when(tile > 0)
        def _():
            halo_down.wait_recv()
            halo_up.wait_send()

        @pl.when(tile < TILES - 1)
        def _():
            halo_up.wait_recv()
            halo_down.wait_send()

        for m in range(MB):
            for d, rs, r in ((0, -1, 0), (1, 1, ROWS - 1)):
                row = halo_r[d, m].astype(F32)
                for cs in (-1, 0, 1):
                    tap = 3 * (rs + 1) + cs + 1
                    taps[m, tap * C:(tap + 1) * C, r * L:(r + 1) * L] = rolled(row, -cs).astype(BF16)

    def forward(m, spans):
        for lo, hi in spans:
            cols = slice(lo * L, hi * L)
            v = dot(wt_v[...], taps[m, :, cols])
            v = v + jnp.concatenate([bcol[...]] * (hi - lo), axis=1)
            v2 = v * v
            t = jnp.tanh(v * (TANH_SCALE * CUBIC_TERM * v2 + TANH_SCALE))
            p = 0.5 * t + 0.5
            out = v * p
            hidden[m, :, cols] = out.astype(BF16)
            slope[m, :, cols] = p + out * (1.0 - p) * (6.0 * TANH_SCALE * CUBIC_TERM * v2 + 2.0 * TANH_SCALE)

    def total_row(m, r):
        return cot_v[m, pl.ds(r, C, stride=ROWS), :] + sg_r[m, r].astype(F32)

    def pre_grads(m):
        land = land_v[...].astype(F32)
        for r in range(ROWS):
            masked[m, :, r * L:(r + 1) * L] = (total_row(m, r) * land[r:r + 1, :]).astype(BF16)

        for j in range(2):
            cols = slice(j * 512, (j + 1) * 512)
            grad = dot(wo_v[...], masked[m, :, cols]) * slope[m, :, cols]
            bias_acc[...] += (grad[:, :L] + grad[:, L:2 * L]) + (grad[:, 2 * L:3 * L] + grad[:, 3 * L:])
            pre[m, :, L + j * 512:L + (j + 1) * 512] = grad.astype(BF16)

    def weight_grads(m, first):
        p = pre[m, :, L:(ROWS + 1) * L]
        for g in range(3):
            term = dot_t(taps[m, g * 384:(g + 1) * 384, :], p)

            @pl.when(first)
            def _():
                w1_acc[g * 384:(g + 1) * 384, :] = term

            @pl.when(jnp.logical_not(first))
            def _():
                w1_acc[g * 384:(g + 1) * 384, :] += term

        term = dot_t(hidden[m], masked[m])

        @pl.when(first)
        def _():
            w2_acc[...] = term

        @pl.when(jnp.logical_not(first))
        def _():
            w2_acc[...] += term

    def gather_steps(acc, lanes):
        return rolled(acc[:C, lanes], -1) + acc[C:2 * C, lanes] + rolled(acc[2 * C:, lanes], 1)

    def conv_edges(m):
        both = dot(w_edge[...], jnp.concatenate([pre[m, :, L:2 * L], pre[m, :, ROWS * L:(ROWS + 1) * L]], axis=1))
        return gather_steps(both[:384], slice(0, L)), gather_steps(both[384:], slice(L, 2 * L))

    def conv_back(m, half):
        starts = [(half * 4 + 1 - rs) * L for rs in (-1, 0, 1)]
        acc = dot(w_cat[...], jnp.concatenate([pre[m, :, s:s + 4 * L] for s in starts], axis=0))
        return [gather_steps(acc, slice(i * L, (i + 1) * L)) for i in range(4)]

    def edges(m):
        up = remote(edge_s.at[m, 0], edge_r.at[m, 1], edge_ss.at[m, 0], edge_rs.at[m, 1], (lead, tile - 1))
        down = remote(edge_s.at[m, 1], edge_r.at[m, 0], edge_ss.at[m, 1], edge_rs.at[m, 0], (lead, tile + 1))
        return up, down

    def sg_copy(m, i):
        rows = pl.ds(*((1, 3), (4, 3), (0, 1), (ROWS - 1, 1))[i])
        return remote(sg_s.at[m, rows], sg_r.at[m, rows], sg_ss.at[m, i], sg_rs.at[m, i], (1 - lead, tile))

    def finish_row(m, r, value):
        out_v[m, pl.ds(r, C, stride=ROWS), :] = value
        sg_s[m, r] = value.astype(BF16)

    def input_grads(m):
        up, down = edges(m)
        edge_s[m, 0], edge_s[m, 1] = conv_edges(m)

        @pl.when(tile > 0)
        def _():
            up.start()

        @pl.when(tile < TILES - 1)
        def _():
            down.start()

        for half in range(2):
            for i, grad in enumerate(conv_back(m, half)):
                r = half * 4 + i
                if r in (0, ROWS - 1):
                    part[m, half] = total_row(m, r) + grad
                else:
                    finish_row(m, r, total_row(m, r) + grad)

            @pl.when(lead == 1)
            def _():
                sg_copy(m, half).start()

    def finish_edges(m):
        up, down = edges(m)
        for d, r in ((0, 0), (1, ROWS - 1)):
            @pl.when(tile > 0 if d == 0 else tile < TILES - 1)
            def _():
                (down if d == 0 else up).wait_recv()
                (up if d == 0 else down).wait_send()
                finish_row(m, r, part[m, d] + edge_r[m, d])

            @pl.when(tile == 0 if d == 0 else tile == TILES - 1)
            def _():
                finish_row(m, r, part[m, d])

            @pl.when(lead == 1)
            def _():
                sg_copy(m, 2 + d).start()

    def piece(b, half):
        return (
            w1_acc[pl.ds(pl.multiple_of(b * 144, 8), 144), pl.ds(pl.multiple_of(half * 256, 256), 256)],
            jnp.concatenate(
                [w2_acc[pl.ds(pl.multiple_of(b * 64 + half * 32 + q * 16, 16), 16), :] for q in range(2)], axis=1
            ),
            jnp.broadcast_to(b_row[:, pl.ds(pl.multiple_of(half * 256, 256), 256)], (16, 256)),
        )

    pair = (lead, tile + 1 - 2 * core)

    def c_copy(k):
        b = lax.rem(block + 1 + k, BLOCKS)
        return b, remote(c_s.at[b], c_r.at[b], c_ss.at[k], c_rs.at[k], pair)

    def y_copy(k):
        b = lax.rem(block + 1 + k, BLOCKS)
        return b, remote(y_s.at[b], y_r.at[k], y_ss.at[k], y_rs.at[k], (lead, b * LOCAL + local))

    def start_core_stage():
        for j in range(4):
            b_row[:, j * 128:(j + 1) * 128] = jnp.sum(bias_acc[j * 128:(j + 1) * 128, :].T, axis=0, keepdims=True)

        def step(k, carry):
            b, copy = c_copy(k)
            one, two, three = piece(b, 1 - core)
            c_s[b, :144, :] = one.astype(BF16)
            c_s[b, 144:160, :] = two.astype(BF16)
            c_s[b, 160:, :] = three.astype(BF16)
            copy.start()
            return carry

        lax.fori_loop(0, BLOCKS, step, 0)

    def sweep(it, carry):
        m = lax.rem(it, MB)
        ahead = it < MB

        @pl.when(ahead)
        def _():
            forward(m, ((0, 2), (6, 8)))

        @pl.when(jnp.where(lead == 1, (it == 1) | (it == MB), it == MB + 1))
        def _():
            finish_edges(1 - m)

        mine = jnp.where(ahead, lead == 1, lead == 0)

        @pl.when(mine)
        def _():
            @pl.when(lead == 0)
            def _():
                for i in range(4):
                    sg_copy(m, i).wait_recv()

            pre_grads(m)

        @pl.when(jnp.logical_not(ahead))
        def _():
            weight_grads(m, it == MB)

        @pl.when(it == 2 * MB - 1)
        def _():
            start_core_stage()

        @pl.when(mine)
        def _():
            input_grads(m)

        return carry

    forward(0, ((2, 6),))
    forward(1, ((2, 6),))
    halo_arrived()
    lax.fori_loop(0, 2 * MB, sweep, 0)

    def y_step(k, carry):
        b, copy = c_copy(k)
        copy.wait_recv()
        for value, lo, hi in zip(piece(b, core), (0, 144, 160), (144, 160, BROWS)):
            value = value + c_r[b, lo:hi, :].astype(F32)
            y_sum[lo:hi, :] = value
            y_s[b, lo:hi, :] = value.astype(BF16)

        @pl.when(k < BLOCKS - 1)
        def _():
            y_copy(k)[1].start()

        return carry

    lax.fori_loop(0, BLOCKS, y_step, 0)

    @pl.when(lead == 0)
    def _():
        finish_edges(MB - 1)

    for k in range(BLOCKS - 1):
        y_copy(k)[1].wait_recv()
        y_sum[...] += y_r[k].astype(F32)

    l_s[...] = y_sum[...].astype(BF16)
    l_copy = remote(l_s, l_r, l_ss, l_rs, (1 - lead, tile))

    @pl.when(lead == 1)
    def _():
        l_copy.start()

    def f_copy(k, which):
        to = lax.rem(local + k, LOCAL)
        return remote(
            f_s.at[to], f_r.at[local], f_ss.at[k, which], f_rs.at[k], (which, block * LOCAL + to)
        )

    def f_landed(k):
        source = lax.rem(local + LOCAL - k, LOCAL)
        return remote(f_s.at[local], f_r.at[source], f_ss.at[k, 0], f_rs.at[k], (1 - lead, tile))

    @pl.when(lead == 0)
    def _():
        l_copy.wait_recv()
        y_sum[...] += l_r[...].astype(F32)
        for j in range(LOCAL):
            f_t[j, :18, :] = y_sum[18 * j:18 * j + 18, :]
            f_t[j, 18:19, :] = y_sum[160:161, :]
            q = (j // 2) % 2
            for i in range(2):
                first = 144 + 8 * (j % 2) + 4 * i
                f_t[j, 19:23, i * L:(i + 1) * L] = y_sum[first:first + 4, q * L:(q + 1) * L]
            f_t[j, 23:24, :] = jnp.zeros((1, 256), F32)
            f_s[j] = f_t[j].astype(BF16)
        for k in range(LOCAL):
            f_copy(k, 1).start()
        for k in range(1, LOCAL):
            f_copy(k, 0).start()
        f_r[local] = f_s[local]

    @pl.when(lead == 1)
    def _():
        f_landed(0).wait_recv()

    for k in range(1, LOCAL):
        f_landed(k).wait_recv()

    for half in range(2):
        total = f_r[half].astype(F32)
        for x in range(1, 4):
            total = total + f_r[2 * x + half].astype(F32)
        total = total * scale
        w1_out[:, half * 256:(half + 1) * 256] = total[:18]
        b_row[:, half * 256:(half + 1) * 256] = total[18:19]
    tail_core = lax.div(xpos, 2)
    total = f_r[tail_core].astype(F32)
    for x in range(1, 4):
        total = total + f_r[2 * x + tail_core].astype(F32)
    total = total * scale
    w2_out[:4, :] = total[19:23, :L]
    w2_out[4:, :] = total[19:23, L:]
    b1 = b_row[:, :L]
    for q in range(1, 4):
        b1 = jnp.where(lax.div(tile, 16) == q, b_row[:, q * L:(q + 1) * L], b1)
    b1_out[...] = pltpu.roll(b1, lax.rem(L - 8 * lax.rem(tile, 16), L), 1)

    @pl.when(lead == 1)
    def _():
        for m in range(MB):
            for i in range(4):
                sg_copy(m, i).wait_send()
        l_copy.wait_send()

    @pl.when(lead == 0)
    def _():
        for k in range(LOCAL):
            f_copy(k, 1).wait_send()
        for k in range(1, LOCAL):
            f_copy(k, 0).wait_send()

    for k in range(BLOCKS):
        c_copy(k)[1].wait_send()
    for k in range(BLOCKS - 1):
        y_copy(k)[1].wait_send()


def deliver(*refs):
    held, outs, b1_own, sems = refs[:4], refs[4:8], refs[8], refs[9]
    b1_own[...] = held[3][0, :8]
    held = held[:3] + (b1_own,)
    copies = [pltpu.make_async_copy(src, dst, sems.at[i]) for i, (src, dst) in enumerate(zip(held, outs))]
    for copy in copies:
        copy.start()
    for copy in copies:
        copy.wait()


def shards(states, cotangents, w_conv, b_conv, w_out, forcing, land, dates):
    grad_scale = 1.0 / math.sqrt(2 * MB * TILES * ROWS * L)
    any_spec = pl.BlockSpec(memory_space=pl.ANY)
    vmem_spec = pl.BlockSpec(memory_space=pltpu.VMEM)
    dma = pltpu.SemaphoreType.DMA
    flat = (MB, C * ROWS, L)
    out, w1, w2, b1 = pl.pallas_call(
        functools.partial(kernel, grad_scale),
        out_shape=(
            pltpu.VMEM(flat, F32),
            pltpu.VMEM((18, H), F32),
            pltpu.VMEM((8, C), F32),
            pltpu.VMEM((1, L), F32),
        ),
        in_specs=[pl.BlockSpec(memory_space=pltpu.SMEM)] + [any_spec] * 7,
        out_specs=(vmem_spec, vmem_spec, vmem_spec, vmem_spec),
        scratch_shapes=[
            pltpu.VMEM(flat, F32),
            pltpu.VMEM(flat, F32),
            pltpu.VMEM((9 * C, H), BF16),
            pltpu.VMEM((H, 9 * C), BF16),
            pltpu.VMEM((3 * C, 3 * H), BF16),
            pltpu.VMEM((6 * C, H), BF16),
            pltpu.VMEM((1, H), F32),
            pltpu.VMEM((H, C), BF16),
            pltpu.VMEM(forcing.shape, F32),
            pltpu.VMEM((ROWS, L), jnp.int32),
            pltpu.VMEM((H, L), F32),
            pltpu.VMEM((MB, C, L), F32),
            pltpu.VMEM((MB, 9 * C, ROWS * L), BF16),
            pltpu.VMEM((2, MB, C, L), BF16),
            pltpu.VMEM((2, MB, C, L), BF16),
            pltpu.VMEM((MB, H, ROWS * L), BF16),
            pltpu.VMEM((MB, H, ROWS * L), F32),
            pltpu.VMEM((MB, C, ROWS * L), BF16),
            pltpu.VMEM((MB, H, (ROWS + 2) * L), BF16),
            pltpu.VMEM((H, L), F32),
            pltpu.VMEM((MB, 2, C, L), F32),
            pltpu.VMEM((MB, 2, C, L), F32),
            pltpu.VMEM((MB, 2, C, L), F32),
            pltpu.VMEM((MB, ROWS, C, L), BF16),
            pltpu.VMEM((MB, ROWS, C, L), BF16),
            pltpu.VMEM((9 * C, H), F32),
            pltpu.VMEM((H, C), F32),
            pltpu.VMEM((1, H), F32),
            pltpu.VMEM((BLOCKS, BROWS, 256), BF16),
            pltpu.VMEM((BLOCKS, BROWS, 256), BF16),
            pltpu.VMEM((BLOCKS, BROWS, 256), BF16),
            pltpu.VMEM((BLOCKS - 1, BROWS, 256), BF16),
            pltpu.VMEM((BROWS, 256), F32),
            pltpu.VMEM((LOCAL, 24, 256), F32),
            pltpu.VMEM((LOCAL, 24, 256), BF16),
            pltpu.VMEM((LOCAL, 24, 256), BF16),
            pltpu.VMEM((BROWS, 256), BF16),
            pltpu.VMEM((BROWS, 256), BF16),
            dma((7,)), dma((2,)), dma((2,)), dma((MB, 2)), dma((MB, 2)), dma((MB, 4)), dma((MB, 4)),
            dma((BLOCKS,)), dma((BLOCKS,)), dma((BLOCKS - 1,)), dma((BLOCKS - 1,)), dma((LOCAL, 2)), dma((LOCAL,)), dma, dma,
        ],
        compiler_params=pltpu.CompilerParams(collective_id=0, has_side_effects=True, vmem_limit_bytes=56 << 20),
    )(
        dates,
        states.reshape(flat),
        cotangents.reshape(flat),
        w_conv,
        b_conv.reshape(1, H),
        w_out,
        forcing,
        land,
    )
    out, w1, w2, b1 = pl.pallas_call(
        deliver,
        out_shape=(
            jax.ShapeDtypeStruct(flat, F32),
            jax.ShapeDtypeStruct((18, H), F32),
            jax.ShapeDtypeStruct((8, C), F32),
            jax.ShapeDtypeStruct((8,), F32),
        ),
        in_specs=[vmem_spec] * 4,
        out_specs=(any_spec,) * 4,
        scratch_shapes=[pltpu.VMEM((8,), F32), dma((4,))],
    )(*(pltpu.with_memory_space_constraint(value, pltpu.VMEM) for value in (out, w1, w2, b1)))
    return out.reshape(states.shape), w1, w2, b1


def solution(mesh):
    placed = (
        P("lead", None, None, "tile", None),
        P("lead", None, None, "tile", None),
        P(),
        P(),
        P(),
        P(),
        P("tile", None),
        P(),
    )
    return jax.shard_map(
        shards,
        mesh=mesh,
        in_specs=placed,
        out_specs=(
            P("lead", None, None, "tile", None),
            P("tile", None),
            P("tile", None),
            P("tile"),
        ),
        check_vma=False,
    )
```

time: 65.3 us -> 55 us (0.84)
  the two profiles are of different devices: /device:TPU:96 before, /device:TPU:1 now
where the time goes in v1:
time: 55 us; the launch traced here: 54.6 us
  Pallas kernels  53.9 us (98%)
  between operations  0.64 us (1%)
    pallas_call x1, Pallas kernels, shards(): pl.pallas_call(functools.partial(kernel, grad_scale), out_shape=(pltpu.VM...  52.9 us

profile of v1, /device:TPU:1, one launch (start us, length us, event | category | flops | bytes accessed | tf_op | source)
XLA Modules:
  0.0 54.6 jit_solution(6396111534956567678)
XLA Ops:
  0.6 52.9 %shard_map.111 = (f32[2,1024,128]{2,1,0:T(8,128)S(1)}, f32[18,512]{1,0:T(8,128)S(1)}, f32[8,128]{1,0:T(8,128)S(1)}, f32[1,128]{1,0:T(1,128)S(1)}) custom-call(s32[2]{0:T(128)} %dates.1, f32[2,1024,128]{2,1,0:T(8,128)} %bitcast.4, f32[2,1024,128]{2,1,0:T(8,128)} %bitcast.5, bf16[1152,512]{1,0:T(8,128)(2,1)} %w_hbm.1, f32[1,512]{1,0:T(1,128)} %bitcast.6, ...), custom_call_target="tpu_custom_call" | custom-call | tf_op jit(solution)/shard_map/pallas_call | solution.py:473
  53.6 1.0 %shard_map.112 = (f32[2,1024,128]{2,1,0:T(8,128)}, f32[18,512]{1,0:T(8,128)}, f32[8,128]{1,0:T(8,128)}, f32[8]{0:T(128)}) custom-call(f32[2,1024,128]{2,1,0:T(8,128)S(1)} %get-tuple-element.12.refs_0_, f32[18,512]{1,0:T(8,128)S(1)} %get-tuple-element.13.refs_1_, f32[8,128]{1,0:T(8,128)S(1)} %get-tuple-element.14.refs_2_, f32[1,128]{1,0:T(1,128)S(1)} %get-tuple-element.15.refs_3_), custom_call_target="tpu_custom_call" | custom-call | tf_op jit(solution)/shard_map/pallas_call | solution.py:536

commit v2 on v1

--- a/solution.py
+++ b/solution.py
@@ -22,7 +22,7 @@
 TILES = 64
 BLOCKS = 8
 LOCAL = 8
-BROWS = 176
+BROWS = 168
 
 
 def remote(src, dst, send_sem, recv_sem, device):
@@ -108,24 +108,12 @@
         if rs != 1:
             w_edge[rs // 2 * 384:(rs // 2 + 1) * 384, :] = w_v[rs * 384:(rs + 1) * 384, :]
     pl.semaphore_wait(barrier, len(peers))
-    halo_up = remote(halo_s.at[0], halo_r.at[1], halo_ss.at[0], halo_rs.at[1], (lead, tile - 1))
-    halo_down = remote(halo_s.at[1], halo_r.at[0], halo_ss.at[1], halo_rs.at[0], (lead, tile + 1))
-
-    @pl.when(tile > 0)
-    def _():
-        halo_up.start()
-
-    @pl.when(tile < TILES - 1)
-    def _():
-        halo_down.start()
-
-    @pl.when(tile == 0)
-    def _():
-        halo_r[0] = jnp.zeros_like(halo_r[0])
-
-    @pl.when(tile == TILES - 1)
-    def _():
-        halo_r[1] = jnp.zeros_like(halo_r[1])
+    above, below = (lead, lax.rem(tile + TILES - 1, TILES)), (lead, lax.rem(tile + 1, TILES))
+    inside = (tile > 0, tile < TILES - 1)
+    halo_up = remote(halo_s.at[0], halo_r.at[1], halo_ss.at[0], halo_rs.at[1], above)
+    halo_down = remote(halo_s.at[1], halo_r.at[0], halo_ss.at[1], halo_rs.at[0], below)
+    halo_up.start()
+    halo_down.start()
 
     for lanes in (slice(0, L), slice((ROWS + 1) * L, (ROWS + 2) * L)):
         pre[:, :, lanes] = jnp.zeros((MB, H, L), BF16)
@@ -139,19 +127,11 @@
         load.wait()
 
     def halo_arrived():
-        @pl.when(tile > 0)
-        def _():
-            halo_down.wait_recv()
-            halo_up.wait_send()
-
-        @pl.when(tile < TILES - 1)
-        def _():
-            halo_up.wait_recv()
-            halo_down.wait_send()
-
+        halo_up.wait()
+        halo_down.wait()
         for m in range(MB):
             for d, rs, r in ((0, -1, 0), (1, 1, ROWS - 1)):
-                row = halo_r[d, m].astype(F32)
+                row = jnp.where(inside[d], halo_r[d, m].astype(F32), 0.0)
                 for cs in (-1, 0, 1):
                     tap = 3 * (rs + 1) + cs + 1
                     taps[m, tap * C:(tap + 1) * C, r * L:(r + 1) * L] = rolled(row, -cs).astype(BF16)
@@ -171,39 +151,31 @@
     def total_row(m, r):
         return cot_v[m, pl.ds(r, C, stride=ROWS), :] + sg_r[m, r].astype(F32)
 
-    def pre_grads(m):
+    def pre_grads(m, spans):
         land = land_v[...].astype(F32)
-        for r in range(ROWS):
-            masked[m, :, r * L:(r + 1) * L] = (total_row(m, r) * land[r:r + 1, :]).astype(BF16)
-
-        for j in range(2):
-            cols = slice(j * 512, (j + 1) * 512)
+        for lo, hi in spans:
+            for r in range(lo, hi):
+                masked[m, :, r * L:(r + 1) * L] = (total_row(m, r) * land[r:r + 1, :]).astype(BF16)
+            cols = slice(lo * L, hi * L)
             grad = dot(wo_v[...], masked[m, :, cols]) * slope[m, :, cols]
-            bias_acc[...] += (grad[:, :L] + grad[:, L:2 * L]) + (grad[:, 2 * L:3 * L] + grad[:, 3 * L:])
-            pre[m, :, L + j * 512:L + (j + 1) * 512] = grad.astype(BF16)
-
-    def weight_grads(m, first):
-        p = pre[m, :, L:(ROWS + 1) * L]
+            sums = [grad[:, i * L:(i + 1) * L] for i in range(hi - lo)]
+            while len(sums) > 1:
+                sums = [a + b for a, b in zip(sums[::2], sums[1::2])] + sums[len(sums) // 2 * 2:]
+            bias_acc[...] += sums[0]
+            pre[m, :, (lo + 1) * L:(hi + 1) * L] = grad.astype(BF16)
+
+    def columns(ref, members, rows, spans, offset):
+        parts = [ref[m, rows, (lo + offset) * L:(hi + offset) * L] for m in members for lo, hi in spans]
+        return parts[0] if len(parts) == 1 else jnp.concatenate(parts, axis=1)
+
+    def weight_grads(members, spans, first):
+        p = columns(pre, members, slice(None), spans, 1)
         for g in range(3):
-            term = dot_t(taps[m, g * 384:(g + 1) * 384, :], p)
-
-            @pl.when(first)
-            def _():
-                w1_acc[g * 384:(g + 1) * 384, :] = term
-
-            @pl.when(jnp.logical_not(first))
-            def _():
-                w1_acc[g * 384:(g + 1) * 384, :] += term
-
-        term = dot_t(hidden[m], masked[m])
-
-        @pl.when(first)
-        def _():
-            w2_acc[...] = term
-
-        @pl.when(jnp.logical_not(first))
-        def _():
-            w2_acc[...] += term
+            rows = slice(g * 384, (g + 1) * 384)
+            term = dot_t(columns(taps, members, rows, spans, 0), p)
+            w1_acc[rows, :] = term if first else w1_acc[rows, :] + term
+        term = dot_t(columns(hidden, members, slice(None), spans, 0), columns(masked, members, slice(None), spans, 0))
+        w2_acc[...] = term if first else w2_acc[...] + term
 
     def gather_steps(acc, lanes):
         return rolled(acc[:C, lanes], -1) + acc[C:2 * C, lanes] + rolled(acc[2 * C:, lanes], 1)
@@ -212,64 +184,42 @@
         both = dot(w_edge[...], jnp.concatenate([pre[m, :, L:2 * L], pre[m, :, ROWS * L:(ROWS + 1) * L]], axis=1))
         return gather_steps(both[:384], slice(0, L)), gather_steps(both[384:], slice(L, 2 * L))
 
-    def conv_back(m, half):
-        starts = [(half * 4 + 1 - rs) * L for rs in (-1, 0, 1)]
-        acc = dot(w_cat[...], jnp.concatenate([pre[m, :, s:s + 4 * L] for s in starts], axis=0))
-        return [gather_steps(acc, slice(i * L, (i + 1) * L)) for i in range(4)]
+    def conv_back(m, spans):
+        sides = [columns(pre, (m,), slice(None), spans, 1 - rs) for rs in (-1, 0, 1)]
+        acc = dot(w_cat[...], jnp.concatenate(sides, axis=0))
+        rows = [r for lo, hi in spans for r in range(lo, hi)]
+        return [(r, gather_steps(acc, slice(i * L, (i + 1) * L))) for i, r in enumerate(rows)]
 
     def edges(m):
-        up = remote(edge_s.at[m, 0], edge_r.at[m, 1], edge_ss.at[m, 0], edge_rs.at[m, 1], (lead, tile - 1))
-        down = remote(edge_s.at[m, 1], edge_r.at[m, 0], edge_ss.at[m, 1], edge_rs.at[m, 0], (lead, tile + 1))
+        up = remote(edge_s.at[m, 0], edge_r.at[m, 1], edge_ss.at[m, 0], edge_rs.at[m, 1], above)
+        down = remote(edge_s.at[m, 1], edge_r.at[m, 0], edge_ss.at[m, 1], edge_rs.at[m, 0], below)
         return up, down
 
     def sg_copy(m, i):
-        rows = pl.ds(*((1, 3), (4, 3), (0, 1), (ROWS - 1, 1))[i])
+        rows = pl.ds(*((3, 2), (1, 2), (5, 2), (0, 1), (ROWS - 1, 1))[i])
         return remote(sg_s.at[m, rows], sg_r.at[m, rows], sg_ss.at[m, i], sg_rs.at[m, i], (1 - lead, tile))
 
     def finish_row(m, r, value):
         out_v[m, pl.ds(r, C, stride=ROWS), :] = value
         sg_s[m, r] = value.astype(BF16)
 
-    def input_grads(m):
-        up, down = edges(m)
+    def send_edges(m):
         edge_s[m, 0], edge_s[m, 1] = conv_edges(m)
-
-        @pl.when(tile > 0)
-        def _():
-            up.start()
-
-        @pl.when(tile < TILES - 1)
-        def _():
-            down.start()
-
-        for half in range(2):
-            for i, grad in enumerate(conv_back(m, half)):
-                r = half * 4 + i
-                if r in (0, ROWS - 1):
-                    part[m, half] = total_row(m, r) + grad
-                else:
-                    finish_row(m, r, total_row(m, r) + grad)
-
-            @pl.when(lead == 1)
-            def _():
-                sg_copy(m, half).start()
+        for copy in edges(m):
+            copy.start()
+
+    def input_grads(m, spans):
+        for r, grad in conv_back(m, spans):
+            if r in (0, ROWS - 1):
+                part[m, r // (ROWS - 1)] = total_row(m, r) + grad
+            else:
+                finish_row(m, r, total_row(m, r) + grad)
 
     def finish_edges(m):
-        up, down = edges(m)
+        for copy in edges(m):
+            copy.wait()
         for d, r in ((0, 0), (1, ROWS - 1)):
-            @pl.when(tile > 0 if d == 0 else tile < TILES - 1)
-            def _():
-                (down if d == 0 else up).wait_recv()
-                (up if d == 0 else down).wait_send()
-                finish_row(m, r, part[m, d] + edge_r[m, d])
-
-            @pl.when(tile == 0 if d == 0 else tile == TILES - 1)
-            def _():
-                finish_row(m, r, part[m, d])
-
-            @pl.when(lead == 1)
-            def _():
-                sg_copy(m, 2 + d).start()
+            finish_row(m, r, part[m, d] + jnp.where(inside[d], edge_r[m, d], 0.0))
 
     def piece(b, half):
         return (
@@ -277,7 +227,7 @@
             jnp.concatenate(
                 [w2_acc[pl.ds(pl.multiple_of(b * 64 + half * 32 + q * 16, 16), 16), :] for q in range(2)], axis=1
             ),
-            jnp.broadcast_to(b_row[:, pl.ds(pl.multiple_of(half * 256, 256), 256)], (16, 256)),
+            jnp.broadcast_to(b_row[:, pl.ds(pl.multiple_of(half * 256, 256), 256)], (8, 256)),
         )
 
     pair = (lead, tile + 1 - 2 * core)
@@ -294,78 +244,85 @@
         for j in range(4):
             b_row[:, j * 128:(j + 1) * 128] = jnp.sum(bias_acc[j * 128:(j + 1) * 128, :].T, axis=0, keepdims=True)
 
-        def step(k, carry):
+        for k in range(BLOCKS):
             b, copy = c_copy(k)
             one, two, three = piece(b, 1 - core)
             c_s[b, :144, :] = one.astype(BF16)
             c_s[b, 144:160, :] = two.astype(BF16)
             c_s[b, 160:, :] = three.astype(BF16)
             copy.start()
-            return carry
-
-        lax.fori_loop(0, BLOCKS, step, 0)
-
-    def sweep(it, carry):
-        m = lax.rem(it, MB)
-        ahead = it < MB
-
-        @pl.when(ahead)
-        def _():
-            forward(m, ((0, 2), (6, 8)))
-
-        @pl.when(jnp.where(lead == 1, (it == 1) | (it == MB), it == MB + 1))
-        def _():
-            finish_edges(1 - m)
-
-        mine = jnp.where(ahead, lead == 1, lead == 0)
-
-        @pl.when(mine)
-        def _():
-            @pl.when(lead == 0)
-            def _():
-                for i in range(4):
-                    sg_copy(m, i).wait_recv()
-
-            pre_grads(m)
-
-        @pl.when(jnp.logical_not(ahead))
-        def _():
-            weight_grads(m, it == MB)
-
-        @pl.when(it == 2 * MB - 1)
-        def _():
-            start_core_stage()
-
-        @pl.when(mine)
-        def _():
-            input_grads(m)
-
-        return carry
-
-    forward(0, ((2, 6),))
-    forward(1, ((2, 6),))
-    halo_arrived()
-    lax.fori_loop(0, 2 * MB, sweep, 0)
-
-    def y_step(k, carry):
+
+    inner, outer, whole = ((2, 6),), ((0, 2), (6, 8)), ((0, 4), (4, 8))
+    most, ends = ((1, 7),), ((0, 1), (7, 8))
+
+    @pl.when(lead == 1)
+    def _():
+        for m in range(MB):
+            forward(m, inner)
+            pre_grads(m, inner)
+            input_grads(m, ((3, 5),))
+            sg_copy(m, 0).start()
+        halo_arrived()
+        for m in range(MB):
+            forward(m, outer)
+            pre_grads(m, outer)
+            input_grads(m, ((1, 3), (5, 7)))
+            for i in (1, 2):
+                sg_copy(m, i).start()
+            send_edges(m)
+        for m in range(MB):
+            input_grads(m, ends)
+        for m in range(MB):
+            finish_edges(m)
+            for i in (3, 4):
+                sg_copy(m, i).start()
+        for m in range(MB):
+            weight_grads((m,), ((0, 8),), m == 0)
+
+    @pl.when(lead == 0)
+    def _():
+        for m in range(MB):
+            forward(m, inner)
+        halo_arrived()
+        for m in range(MB):
+            forward(m, outer)
+        for m in range(MB):
+            for i in range(3):
+                sg_copy(m, i).wait_recv()
+            pre_grads(m, most)
+            weight_grads((m,), most, m == 0)
+        for m in range(MB):
+            for i in (3, 4):
+                sg_copy(m, i).wait_recv()
+            pre_grads(m, ends)
+        weight_grads((0, 1), ends, False)
+
+    start_core_stage()
+
+    @pl.when(lead == 0)
+    def _():
+        for m in range(MB):
+            send_edges(m)
+
+    for k in range(BLOCKS):
         b, copy = c_copy(k)
         copy.wait_recv()
         for value, lo, hi in zip(piece(b, core), (0, 144, 160), (144, 160, BROWS)):
             value = value + c_r[b, lo:hi, :].astype(F32)
-            y_sum[lo:hi, :] = value
-            y_s[b, lo:hi, :] = value.astype(BF16)
-
-        @pl.when(k < BLOCKS - 1)
-        def _():
+            if k < BLOCKS - 1:
+                y_s[b, lo:hi, :] = value.astype(BF16)
+            else:
+                y_sum[lo:hi, :] = value
+        if k < BLOCKS - 1:
             y_copy(k)[1].start()
 
-        return carry
-
-    lax.fori_loop(0, BLOCKS, y_step, 0)
-
     @pl.when(lead == 0)
     def _():
-        finish_edges(MB - 1)
+        for m in range(MB):
+            for span in whole:
+                input_grads(m, (span,))
+        for m in range(MB):
+            finish_edges(m)
 
     for k in range(BLOCKS - 1):
         y_copy(k)[1].wait_recv()
@@ -436,7 +393,7 @@
     @pl.when(lead == 1)
     def _():
         for m in range(MB):
-            for i in range(4):
+            for i in range(5):
                 sg_copy(m, i).wait_send()
         l_copy.wait_send()
 
@@ -519,7 +476,7 @@
             pltpu.VMEM((LOCAL, 24, 256), BF16),
             pltpu.VMEM((BROWS, 256), BF16),
             pltpu.VMEM((BROWS, 256), BF16),
-            dma((7,)), dma((2,)), dma((2,)), dma((MB, 2)), dma((MB, 2)), dma((MB, 4)), dma((MB, 4)),
+            dma((7,)), dma((2,)), dma((2,)), dma((MB, 2)), dma((MB, 2)), dma((MB, 5)), dma((MB, 5)),
             dma((BLOCKS,)), dma((BLOCKS,)), dma((BLOCKS - 1,)), dma((BLOCKS - 1,)), dma((LOCAL, 2)), dma((LOCAL,)), dma, dma,
         ],
         compiler_params=pltpu.CompilerParams(collective_id=0, has_side_effects=True, vmem_limit_bytes=56 << 20),

time: 55 us -> 50.2 us (0.913)
  Pallas kernels: 53.9 us -> 49.2 us
    pallas_call x1, Pallas kernels: 52.9 us -> 48.2 us  [shards(): pl.pallas_call(functools.partial(kernel, grad_scale), out_shape=(pltpu.VM...]
where the time goes in v2:
time: 50.2 us; the launch traced here: 50 us
  Pallas kernels  49.2 us (98%)
  between operations  0.8 us (2%)
    pallas_call x1, Pallas kernels, shards(): pl.pallas_call(functools.partial(kernel, grad_scale), out_shape=(pltpu.VM...  48.2 us
    pallas_call x1, Pallas kernels, shards(): pl.pallas_call(deliver, out_shape=(jax.ShapeDtypeStruct(flat, F32), jax.S...  1.01 us

profile of v2, /device:TPU:1, one launch (start us, length us, event | category | flops | bytes accessed | tf_op | source)
XLA Modules:
  0.0 50.0 jit_solution(8491990039196480715)
XLA Ops:
  0.6 48.2 %shard_map.111 = (f32[2,1024,128]{2,1,0:T(8,128)S(1)}, f32[18,512]{1,0:T(8,128)S(1)}, f32[8,128]{1,0:T(8,128)S(1)}, f32[1,128]{1,0:T(1,128)S(1)}) custom-call(s32[2]{0:T(128)} %dates.1, f32[2,1024,128]{2,1,0:T(8,128)} %bitcast.4, f32[2,1024,128]{2,1,0:T(8,128)} %bitcast.5, bf16[1152,512]{1,0:T(8,128)(2,1)} %w_hbm.1, f32[1,512]{1,0:T(1,128)} %bitcast.6, ...), custom_call_target="tpu_custom_call" | custom-call | tf_op jit(solution)/shard_map/pallas_call | solution.py:430
  48.9 1.0 %shard_map.112 = (f32[2,1024,128]{2,1,0:T(8,128)}, f32[18,512]{1,0:T(8,128)}, f32[8,128]{1,0:T(8,128)}, f32[8]{0:T(128)}) custom-call(f32[2,1024,128]{2,1,0:T(8,128)S(1)} %get-tuple-element.12.refs_0_, f32[18,512]{1,0:T(8,128)S(1)} %get-tuple-element.13.refs_1_, f32[8,128]{1,0:T(8,128)S(1)} %get-tuple-element.14.refs_2_, f32[1,128]{1,0:T(1,128)S(1)} %get-tuple-element.15.refs_3_), custom_call_target="tpu_custom_call" | custom-call | tf_op jit(solution)/shard_map/pallas_call | solution.py:493

commit v3 on v2

--- a/solution.py
+++ b/solution.py
@@ -22,7 +22,8 @@
 TILES = 64
 BLOCKS = 8
 LOCAL = 8
-BROWS = 168
+BROWS = 184
+XROWS = 40
 
 
 def remote(src, dst, send_sem, recv_sem, device):
@@ -38,6 +39,10 @@
 
 def dot_t(a, b):
     return lax.dot_general(a, b, (((1,), (1,)), ((), ())), preferred_element_type=F32)
+
+
+def aligned(index, size):
+    return index if isinstance(index, int) else pl.multiple_of(index, size)
 
 
 def rolled(value, shift):
@@ -51,9 +56,9 @@
     x_v, cot_v, w_v, wt_v, w_cat, w_edge, b_v, wo_v, f_v, land_v,
     bcol, shift, taps, halo_s, halo_r, hidden, slope, masked, pre, bias_acc,
     edge_s, edge_r, part, sg_s, sg_r, w1_acc, w2_acc, b_row,
-    c_s, c_r, y_s, y_r, y_sum, f_t, f_s, f_r, l_s, l_r,
+    c_s, c_r, y_s, y_r, y_sum, f_t, f_s, f_r, l0_s, l0_r, x_s, x_r, x_t, g_s, g_r, l1_s, l1_r,
     in_sem, halo_ss, halo_rs, edge_ss, edge_rs, sg_ss, sg_rs,
-    c_ss, c_rs, y_ss, y_rs, f_ss, f_rs, l_ss, l_rs,
+    c_ss, c_rs, y_ss, y_rs, f_ss, f_rs, x_ss, x_rs, g_ss, g_rs, l_ss, l_rs,
 ):
     lead = lax.axis_index("lead")
     tile = lax.axis_index("tile")
@@ -61,13 +66,6 @@
     local = lax.rem(tile, LOCAL)
     block = lax.div(tile, LOCAL)
     xpos = lax.div(local, 2)
-
-    peers = [(lead, lax.rem(tile + 1, TILES)), (lead, lax.rem(tile + TILES - 1, TILES)), (1 - lead, tile)]
-    peers += [(lead, lax.rem(block + k, BLOCKS) * LOCAL + local) for k in range(1, BLOCKS)]
-    peers += [(which, block * LOCAL + lax.rem(local + k, LOCAL)) for k in range(1, LOCAL) for which in (lead, 1 - lead)]
-    barrier = pltpu.get_barrier_semaphore()
-    for peer in peers:
-        pl.semaphore_signal(barrier, inc=1, device_id=peer, device_id_type=MESH)
 
     loads = [
         pltpu.make_async_copy(src, dst, in_sem.at[i])
@@ -77,6 +75,14 @@
     ]
     for load in loads:
         load.start()
+
+    peers = [(lead, lax.rem(tile + 1, TILES)), (lead, lax.rem(tile + TILES - 1, TILES)), (1 - lead, tile)]
+    others = [lax.rem(block + k, BLOCKS) * LOCAL + 2 * xpos + c for k in range(1, BLOCKS) for c in range(2)]
+    others += [block * LOCAL + lax.rem(local + k, LOCAL) for k in range(1, LOCAL)]
+    peers += [(which, other) for other in others for which in (lead, 1 - lead)]
+    barrier = pltpu.get_barrier_semaphore()
+    for peer in peers:
+        pl.semaphore_signal(barrier, inc=1, device_id=peer, device_id_type=MESH)
 
     loads[0].wait()
     for m in range(MB):
@@ -168,14 +174,20 @@
         parts = [ref[m, rows, (lo + offset) * L:(hi + offset) * L] for m in members for lo, hi in spans]
         return parts[0] if len(parts) == 1 else jnp.concatenate(parts, axis=1)
 
-    def weight_grads(members, spans, first):
+    def weight_grads(members, spans, first, last=False):
+        term = dot_t(columns(hidden, members, slice(None), spans, 0), columns(masked, members, slice(None), spans, 0))
+        w2_acc[...] = term if first else w2_acc[...] + term
+        if last:
+            for j in range(4):
+                b_row[:, j * 128:(j + 1) * 128] = jnp.sum(bias_acc[j * 128:(j + 1) * 128, :].T, axis=0, keepdims=True)
         p = columns(pre, members, slice(None), spans, 1)
-        for g in range(3):
-            rows = slice(g * 384, (g + 1) * 384)
+        for lo, hi in ((0, 3), (3, 6), (6, 8)):
+            rows = slice(lo * 144, hi * 144)
             term = dot_t(columns(taps, members, rows, spans, 0), p)
             w1_acc[rows, :] = term if first else w1_acc[rows, :] + term
-        term = dot_t(columns(hidden, members, slice(None), spans, 0), columns(masked, members, slice(None), spans, 0))
-        w2_acc[...] = term if first else w2_acc[...] + term
+            if last:
+                for b in range(lo, hi):
+                    start_core_stage(b)
 
     def gather_steps(acc, lanes):
         return rolled(acc[:C, lanes], -1) + acc[C:2 * C, lanes] + rolled(acc[2 * C:, lanes], 1)
@@ -222,35 +234,32 @@
             finish_row(m, r, part[m, d] + jnp.where(inside[d], edge_r[m, d], 0.0))
 
     def piece(b, half):
+        first = b * 64
         return (
-            w1_acc[pl.ds(pl.multiple_of(b * 144, 8), 144), pl.ds(pl.multiple_of(half * 256, 256), 256)],
+            w1_acc[pl.ds(aligned(b * 144, 8), 144), pl.ds(pl.multiple_of(half * 256, 256), 256)],
             jnp.concatenate(
-                [w2_acc[pl.ds(pl.multiple_of(b * 64 + half * 32 + q * 16, 16), 16), :] for q in range(2)], axis=1
+                [
+                    jnp.concatenate([w2_acc[pl.ds(aligned(first + 32 * i + 16 * q, 16), 16), :] for i in range(2)], axis=0)
+                    for q in range(2)
+                ],
+                axis=1,
             ),
             jnp.broadcast_to(b_row[:, pl.ds(pl.multiple_of(half * 256, 256), 256)], (8, 256)),
         )
 
     pair = (lead, tile + 1 - 2 * core)
 
-    def c_copy(k):
-        b = lax.rem(block + 1 + k, BLOCKS)
-        return b, remote(c_s.at[b], c_r.at[b], c_ss.at[k], c_rs.at[k], pair)
+    def c_copy(b):
+        return remote(c_s.at[b], c_r.at[b], c_ss.at[b], c_rs.at[b], pair)
 
     def y_copy(k):
         b = lax.rem(block + 1 + k, BLOCKS)
         return b, remote(y_s.at[b], y_r.at[k], y_ss.at[k], y_rs.at[k], (lead, b * LOCAL + local))
 
-    def start_core_stage():
-        for j in range(4):
-            b_row[:, j * 128:(j + 1) * 128] = jnp.sum(bias_acc[j * 128:(j + 1) * 128, :].T, axis=0, keepdims=True)
-
-        for k in range(BLOCKS):
-            b, copy = c_copy(k)
-            one, two, three = piece(b, 1 - core)
-            c_s[b, :144, :] = one.astype(BF16)
-            c_s[b, 144:160, :] = two.astype(BF16)
-            c_s[b, 160:, :] = three.astype(BF16)
-            copy.start()
+    def start_core_stage(b):
+        for value, lo, hi in zip(piece(b, 1 - core), (0, 144, 176), (144, 176, BROWS)):
+            c_s[b, lo:hi, :] = value.astype(BF16)
+        c_copy(b).start()
 
     inner, outer, whole = ((2, 6),), ((0, 2), (6, 8)), ((0, 4), (4, 8))
     most, ends = ((1, 7),), ((0, 1), (7, 8))
@@ -266,10 +275,13 @@
         for m in range(MB):
             forward(m, outer)
             pre_grads(m, outer)
+            if m == MB - 1:
+                send_edges(m)
             input_grads(m, ((1, 3), (5, 7)))
             for i in (1, 2):
                 sg_copy(m, i).start()
-            send_edges(m)
+            if m < MB - 1:
+                send_edges(m)
         for m in range(MB):
             input_grads(m, ends)
         for m in range(MB):
@@ -277,7 +289,7 @@
             for i in (3, 4):
                 sg_copy(m, i).start()
         for m in range(MB):
-            weight_grads((m,), ((0, 8),), m == 0)
+            weight_grads((m,), ((0, 8),), m == 0, m == MB - 1)
 
     @pl.when(lead == 0)
     def _():
@@ -295,26 +307,46 @@
             for i in (3, 4):
                 sg_copy(m, i).wait_recv()
             pre_grads(m, ends)
-        weight_grads((0, 1), ends, False)
-
-    start_core_stage()
+        weight_grads((0, 1), ends, False, True)
 
     @pl.when(lead == 0)
     def _():
         for m in range(MB):
             send_edges(m)
 
-    for k in range(BLOCKS):
-        b, copy = c_copy(k)
-        copy.wait_recv()
-        for value, lo, hi in zip(piece(b, core), (0, 144, 160), (144, 160, BROWS)):
-            value = value + c_r[b, lo:hi, :].astype(F32)
+    def x_copy(k):
+        to = lax.rem(xpos + k, 4)
+        return remote(x_s.at[to], x_r.at[k - 1], x_ss.at[k - 1], x_rs.at[k - 1], (lead, block * LOCAL + 2 * to + 1))
+
+    xrow_id = lax.broadcasted_iota(jnp.int32, (XROWS, 256), 0)
+    row_id = lax.broadcasted_iota(jnp.int32, (24, 256), 0)
+
+    @pl.when(core == 0)
+    def _():
+        for k in range(BLOCKS):
+            b = lax.rem(block + 1 + k, BLOCKS)
+            c_copy(b).wait_recv()
+            for value, lo, hi in zip(piece(b, 0), (0, 144, 176), (144, 176, BROWS)):
+                value = value + c_r[b, lo:hi, :].astype(F32)
+                if k < BLOCKS - 1:
+                    y_s[b, lo:hi, :] = value.astype(BF16)
+                else:
+                    y_sum[lo:hi, :] = value
             if k < BLOCKS - 1:
-                y_s[b, lo:hi, :] = value.astype(BF16)
-            else:
-                y_sum[lo:hi, :] = value
-        if k < BLOCKS - 1:
-            y_copy(k)[1].start()
+                y_copy(k)[1].start()
+
+    @pl.when(core == 1)
+    def _():
+        for b in range(BLOCKS):
+            c_copy(b).wait_recv()
+            w1_part, _, bias = piece(b, 1)
+            x_t[b, :144, :] = w1_part + c_r[b, :144, :].astype(F32)
+            x_t[b, 144:152, :] = bias + c_r[b, 176:, :].astype(F32)
+            for x in range(4):
+                rows = jnp.where(xrow_id == 36, x_t[b, 144:145, :], x_t[b, 36 * x:36 * x + XROWS, :])
+                x_s[x, b] = rows.astype(BF16)
+        for k in (2, 1, 3):
+            x_copy(k).start()
 
     @pl.when(lead == 0)
     def _():
@@ -324,67 +356,116 @@
         for m in range(MB):
             finish_edges(m)
 
-    for k in range(BLOCKS - 1):
-        y_copy(k)[1].wait_recv()
-        y_sum[...] += y_r[k].astype(F32)
-
-    l_s[...] = y_sum[...].astype(BF16)
-    l_copy = remote(l_s, l_r, l_ss, l_rs, (1 - lead, tile))
-
-    @pl.when(lead == 1)
-    def _():
-        l_copy.start()
+    l0_copy = remote(l0_s, l0_r, l_ss.at[0], l_rs.at[0], (1 - lead, tile))
+    l1_copy = remote(l1_s, l1_r, l_ss.at[1], l_rs.at[1], (1 - lead, tile))
 
     def f_copy(k, which):
         to = lax.rem(local + k, LOCAL)
+        return remote(f_s.at[to], f_r.at[xpos], f_ss.at[k, which], f_rs.at[xpos], (which, block * LOCAL + to))
+
+    def g_copy(k, c, which):
+        to = lax.rem(block + k, BLOCKS)
         return remote(
-            f_s.at[to], f_r.at[local], f_ss.at[k, which], f_rs.at[k], (which, block * LOCAL + to)
+            g_s.at[c, to], g_r.at[block], g_ss.at[k, 2 * c + which], g_rs.at[block], (which, to * LOCAL + 2 * xpos + c)
         )
 
+    @pl.when(core == 0)
+    def _():
+        for k in range(BLOCKS - 1):
+            y_copy(k)[1].wait_recv()
+            y_sum[...] += y_r[k].astype(F32)
+
+        @pl.when(lead == 1)
+        def _():
+            l0_s[...] = y_sum[...].astype(BF16)
+            l0_copy.start()
+
+        @pl.when(lead == 0)
+        def _():
+            l0_copy.wait_recv()
+            y_sum[...] += l0_r[...].astype(F32)
+            for j in range(LOCAL):
+                f_t[j, :18, :] = y_sum[18 * j:18 * j + 18, :]
+                f_t[j, 18:19, :] = y_sum[176:177, :]
+                x, c = j // 2, j % 2
+                for i in range(2):
+                    first = 144 + 16 * (x // 2) + 8 * c + 4 * i
+                    f_t[j, 19:23, i * L:(i + 1) * L] = y_sum[first:first + 4, (x % 2) * L:(x % 2 + 1) * L]
+                f_t[j, 23:24, :] = jnp.zeros((1, 256), F32)
+                f_s[j] = f_t[j].astype(BF16)
+            for k in range(LOCAL):
+                f_copy(k, 1).start()
+            for k in range(1, LOCAL):
+                f_copy(k, 0).start()
+            f_r[xpos] = f_s[local]
+
+    @pl.when(core == 1)
+    def _():
+        for k in range(1, 4):
+            x_copy(k).wait_recv()
+        for b in range(BLOCKS):
+            total = x_s[xpos, b].astype(F32)
+            for k in range(3):
+                total = total + x_r[k, b].astype(F32)
+            x_t[b, :XROWS, :] = total
+
+        @pl.when(lead == 1)
+        def _():
+            l1_s[...] = x_t[:, :XROWS, :].astype(BF16)
+            l1_copy.start()
+
+        @pl.when(lead == 0)
+        def _():
+            l1_copy.wait_recv()
+            for b in range(BLOCKS):
+                x_t[b, :XROWS, :] = x_t[b, :XROWS, :] + l1_r[b].astype(F32)
+                for c in range(2):
+                    rows = jnp.where(row_id == 18, x_t[b, 36:37, :], x_t[b, 18 * c:18 * c + 24, :])
+                    g_s[c, b] = rows.astype(BF16)
+            for k in range(BLOCKS):
+                for c in range(2):
+                    g_copy(k, c, 1).start()
+            g_copy(0, 0, 0).start()
+            for k in range(1, BLOCKS):
+                for c in range(2):
+                    g_copy(k, c, 0).start()
+            g_r[block] = g_s[1, block]
+
     def f_landed(k):
-        source = lax.rem(local + LOCAL - k, LOCAL)
-        return remote(f_s.at[local], f_r.at[source], f_ss.at[k, 0], f_rs.at[k], (1 - lead, tile))
-
-    @pl.when(lead == 0)
-    def _():
-        l_copy.wait_recv()
-        y_sum[...] += l_r[...].astype(F32)
-        for j in range(LOCAL):
-            f_t[j, :18, :] = y_sum[18 * j:18 * j + 18, :]
-            f_t[j, 18:19, :] = y_sum[160:161, :]
-            q = (j // 2) % 2
-            for i in range(2):
-                first = 144 + 8 * (j % 2) + 4 * i
-                f_t[j, 19:23, i * L:(i + 1) * L] = y_sum[first:first + 4, q * L:(q + 1) * L]
-            f_t[j, 23:24, :] = jnp.zeros((1, 256), F32)
-            f_s[j] = f_t[j].astype(BF16)
-        for k in range(LOCAL):
-            f_copy(k, 1).start()
-        for k in range(1, LOCAL):
-            f_copy(k, 0).start()
-        f_r[local] = f_s[local]
-
-    @pl.when(lead == 1)
+        source = lax.rem(xpos + k, 4)
+        return remote(f_s.at[0], f_r.at[source], f_ss.at[0, 0], f_rs.at[source], (1 - lead, tile))
+
+    def g_landed(k):
+        source = lax.rem(block + k, BLOCKS)
+        return remote(g_s.at[0, 0], g_r.at[source], g_ss.at[0, 0], g_rs.at[source], (1 - lead, tile))
+
+    @pl.when((lead == 1) | (core == 1))
     def _():
         f_landed(0).wait_recv()
 
-    for k in range(1, LOCAL):
+    @pl.when((lead == 1) | (core == 0))
+    def _():
+        g_landed(0).wait_recv()
+
+    for k in range(1, 4):
         f_landed(k).wait_recv()
-
-    for half in range(2):
-        total = f_r[half].astype(F32)
-        for x in range(1, 4):
-            total = total + f_r[2 * x + half].astype(F32)
-        total = total * scale
-        w1_out[:, half * 256:(half + 1) * 256] = total[:18]
-        b_row[:, half * 256:(half + 1) * 256] = total[18:19]
-    tail_core = lax.div(xpos, 2)
-    total = f_r[tail_core].astype(F32)
+    for k in range(1, BLOCKS):
+        g_landed(k).wait_recv()
+
+    total = f_r[0].astype(F32)
     for x in range(1, 4):
-        total = total + f_r[2 * x + tail_core].astype(F32)
+        total = total + f_r[x].astype(F32)
     total = total * scale
+    w1_out[:, :256] = total[:18]
+    b_row[:, :256] = total[18:19]
     w2_out[:4, :] = total[19:23, :L]
     w2_out[4:, :] = total[19:23, L:]
+    total = g_r[0].astype(F32)
+    for b in range(1, BLOCKS):
+        total = total + g_r[b].astype(F32)
+    total = total * scale
+    w1_out[:, 256:] = total[:18]
+    b_row[:, 256:] = total[18:19]
     b1 = b_row[:, :L]
     for q in range(1, 4):
         b1 = jnp.where(lax.div(tile, 16) == q, b_row[:, q * L:(q + 1) * L], b1)
@@ -395,19 +476,44 @@
         for m in range(MB):
             for i in range(5):
                 sg_copy(m, i).wait_send()
-        l_copy.wait_send()
-
-    @pl.when(lead == 0)
-    def _():
-        for k in range(LOCAL):
-            f_copy(k, 1).wait_send()
-        for k in range(1, LOCAL):
-            f_copy(k, 0).wait_send()
-
-    for k in range(BLOCKS):
-        c_copy(k)[1].wait_send()
-    for k in range(BLOCKS - 1):
-        y_copy(k)[1].wait_send()
+
+    for b in range(BLOCKS):
+        c_copy(b).wait_send()
+
+    @pl.when(core == 0)
+    def _():
+        for k in range(BLOCKS - 1):
+            y_copy(k)[1].wait_send()
+
+        @pl.when(lead == 1)
+        def _():
+            l0_copy.wait_send()
+
+        @pl.when(lead == 0)
+        def _():
+            for k in range(LOCAL):
+                f_copy(k, 1).wait_send()
+            for k in range(1, LOCAL):
+                f_copy(k, 0).wait_send()
+
+    @pl.when(core == 1)
+    def _():
+        for k in range(1, 4):
+            x_copy(k).wait_send()
+
+        @pl.when(lead == 1)
+        def _():
+            l1_copy.wait_send()
+
+        @pl.when(lead == 0)
+        def _():
+            for k in range(BLOCKS):
+                for c in range(2):
+                    g_copy(k, c, 1).wait_send()
+            g_copy(0, 0, 0).wait_send()
+            for k in range(1, BLOCKS):
+                for c in range(2):
+                    g_copy(k, c, 0).wait_send()
 
 
 def deliver(*refs):
@@ -473,11 +579,18 @@
             pltpu.VMEM((BROWS, 256), F32),
             pltpu.VMEM((LOCAL, 24, 256), F32),
             pltpu.VMEM((LOCAL, 24, 256), BF16),
-            pltpu.VMEM((LOCAL, 24, 256), BF16),
+            pltpu.VMEM((4, 24, 256), BF16),
             pltpu.VMEM((BROWS, 256), BF16),
             pltpu.VMEM((BROWS, 256), BF16),
+            pltpu.VMEM((4, BLOCKS, XROWS, 256), BF16),
+            pltpu.VMEM((3, BLOCKS, XROWS, 256), BF16),
+            pltpu.VMEM((BLOCKS, 152, 256), F32),
+            pltpu.VMEM((2, BLOCKS, 24, 256), BF16),
+            pltpu.VMEM((BLOCKS, 24, 256), BF16),
+            pltpu.VMEM((BLOCKS, XROWS, 256), BF16),
+            pltpu.VMEM((BLOCKS, XROWS, 256), BF16),
             dma((7,)), dma((2,)), dma((2,)), dma((MB, 2)), dma((MB, 2)), dma((MB, 5)), dma((MB, 5)),
-            dma((BLOCKS,)), dma((BLOCKS,)), dma((BLOCKS - 1,)), dma((BLOCKS - 1,)), dma((LOCAL, 2)), dma((LOCAL,)), dma, dma,
+            dma((BLOCKS,)), dma((BLOCKS,)), dma((BLOCKS - 1,)), dma((BLOCKS - 1,)), dma((LOCAL, 2)), dma((4,)), dma((3,)), dma((3,)), dma((BLOCKS, 4)), dma((BLOCKS,)), dma((2,)), dma((2,)),
         ],
         compiler_params=pltpu.CompilerParams(collective_id=0, has_side_effects=True, vmem_limit_bytes=56 << 20),
     )(

time: 50.2 us -> 48 us (0.956)
  Pallas kernels: 49.2 us -> 47.1 us
    pallas_call x1, Pallas kernels: 48.2 us -> 46.1 us  [shards(): pl.pallas_call(functools.partial(kernel, grad_scale), out_shape=(pltpu.VM...]
where the time goes in v3:
time: 48 us; the launch traced here: 47.9 us
  Pallas kernels  47.1 us (98%)
  between operations  0.8 us (2%)
    pallas_call x1, Pallas kernels, shards(): pl.pallas_call(functools.partial(kernel, grad_scale), out_shape=(pltpu.VM...  46.1 us
    pallas_call x1, Pallas kernels, shards(): pl.pallas_call(deliver, out_shape=(jax.ShapeDtypeStruct(flat, F32), jax.S...  1.01 us

profile of v3, /device:TPU:1, one launch (start us, length us, event | category | flops | bytes accessed | tf_op | source)
XLA Modules:
  0.0 47.9 jit_solution(9883575145288832560)
XLA Ops:
  0.6 46.1 %shard_map.111 = (f32[2,1024,128]{2,1,0:T(8,128)S(1)}, f32[18,512]{1,0:T(8,128)S(1)}, f32[8,128]{1,0:T(8,128)S(1)}, f32[1,128]{1,0:T(1,128)S(1)}) custom-call(s32[2]{0:T(128)} %dates.1, f32[2,1024,128]{2,1,0:T(8,128)} %bitcast.4, f32[2,1024,128]{2,1,0:T(8,128)} %bitcast.5, bf16[1152,512]{1,0:T(8,128)(2,1)} %w_hbm.1, f32[1,512]{1,0:T(1,128)} %bitcast.6, ...), custom_call_target="tpu_custom_call" | custom-call | tf_op jit(solution)/shard_map/pallas_call | solution.py:536
  46.8 1.0 %shard_map.112 = (f32[2,1024,128]{2,1,0:T(8,128)}, f32[18,512]{1,0:T(8,128)}, f32[8,128]{1,0:T(8,128)}, f32[8]{0:T(128)}) custom-call(f32[2,1024,128]{2,1,0:T(8,128)S(1)} %get-tuple-element.12.refs_0_, f32[18,512]{1,0:T(8,128)S(1)} %get-tuple-element.13.refs_1_, f32[8,128]{1,0:T(8,128)S(1)} %get-tuple-element.14.refs_2_, f32[1,128]{1,0:T(1,128)S(1)} %get-tuple-element.15.refs_3_), custom_call_target="tpu_custom_call" | custom-call | tf_op jit(solution)/shard_map/pallas_call | solution.py:606

commit v4 on v3

--- a/solution.py
+++ b/solution.py
@@ -216,7 +216,8 @@
         sg_s[m, r] = value.astype(BF16)
 
     def send_edges(m):
-        edge_s[m, 0], edge_s[m, 1] = conv_edges(m)
+        for d, row in enumerate(conv_edges(m)):
+            edge_s[m, d] = row.astype(BF16)
         for copy in edges(m):
             copy.start()
 
@@ -231,7 +232,7 @@
         for copy in edges(m):
             copy.wait()
         for d, r in ((0, 0), (1, ROWS - 1)):
-            finish_row(m, r, part[m, d] + jnp.where(inside[d], edge_r[m, d], 0.0))
+            finish_row(m, r, part[m, d] + jnp.where(inside[d], edge_r[m, d].astype(F32), 0.0))
 
     def piece(b, half):
         first = b * 64
@@ -564,8 +565,8 @@
             pltpu.VMEM((MB, C, ROWS * L), BF16),
             pltpu.VMEM((MB, H, (ROWS + 2) * L), BF16),
             pltpu.VMEM((H, L), F32),
-            pltpu.VMEM((MB, 2, C, L), F32),
-            pltpu.VMEM((MB, 2, C, L), F32),
+            pltpu.VMEM((MB, 2, C, L), BF16),
+            pltpu.VMEM((MB, 2, C, L), BF16),
             pltpu.VMEM((MB, 2, C, L), F32),
             pltpu.VMEM((MB, ROWS, C, L), BF16),
             pltpu.VMEM((MB, ROWS, C, L), BF16),

time: 48 us -> 47.7 us (level)
  no operation moved by 1% of the time
where the time goes in v4:
time: 47.7 us; the launch traced here: 47.6 us
  Pallas kernels  46.8 us (98%)
  between operations  0.8 us (2%)
    pallas_call x1, Pallas kernels, shards(): pl.pallas_call(functools.partial(kernel, grad_scale), out_shape=(pltpu.VM...  45.8 us
    pallas_call x1, Pallas kernels, shards(): pl.pallas_call(deliver, out_shape=(jax.ShapeDtypeStruct(flat, F32), jax.S...  1.01 us

profile of v4, /device:TPU:1, one launch (start us, length us, event | category | flops | bytes accessed | tf_op | source)
XLA Modules:
  0.0 47.6 jit_solution(15504854830529286554)
XLA Ops:
  0.6 45.8 %shard_map.111 = (f32[2,1024,128]{2,1,0:T(8,128)S(1)}, f32[18,512]{1,0:T(8,128)S(1)}, f32[8,128]{1,0:T(8,128)S(1)}, f32[1,128]{1,0:T(1,128)S(1)}) custom-call(s32[2]{0:T(128)} %dates.1, f32[2,1024,128]{2,1,0:T(8,128)} %bitcast.4, f32[2,1024,128]{2,1,0:T(8,128)} %bitcast.5, bf16[1152,512]{1,0:T(8,128)(2,1)} %w_hbm.1, f32[1,512]{1,0:T(1,128)} %bitcast.6, ...), custom_call_target="tpu_custom_call" | custom-call | tf_op jit(solution)/shard_map/pallas_call | solution.py:537
  46.4 1.0 %shard_map.112 = (f32[2,1024,128]{2,1,0:T(8,128)}, f32[18,512]{1,0:T(8,128)}, f32[8,128]{1,0:T(8,128)}, f32[8]{0:T(128)}) custom-call(f32[2,1024,128]{2,1,0:T(8,128)S(1)} %get-tuple-element.12.refs_0_, f32[18,512]{1,0:T(8,128)S(1)} %get-tuple-element.13.refs_1_, f32[8,128]{1,0:T(8,128)S(1)} %get-tuple-element.14.refs_2_, f32[1,128]{1,0:T(1,128)S(1)} %get-tuple-element.15.refs_3_), custom_call_target="tpu_custom_call" | custom-call | tf_op jit(solution)/shard_map/pallas_call | solution.py:607
